TPU v7x, 256 devices: a whole 4x4x8 slice. The times are simulated.
256 devices in a mesh: depth: 64 (over z, y_lo, x), tile: 4 (over y_hi, core).
Axes of the slice: x: 4, y: 4 (y_hi: 2, y_lo: 2; y = y_hi * 2 + y_lo), z: 8, core: 2. Of those that a mesh axis runs over, the one named last changes fastest.
Arguments:
- volume: float32 [2, 64, 225, 512], P(None, 'depth', None, 'tile'), may hold values from 0.1 to 5
- kernel: bfloat16 [64, 225, 81, 225], P('depth'), as said below
- measured: float32 [2, 225, 512], P(None, None, 'tile'), may hold values from 0.2 to 5
Outputs:
- updated: float32 [2, 64, 225, 512], P(None, 'depth', None, 'tile')
Inputs may be any that keep to these rules, and one draw needn't show every extreme that they name: `kernel`: kernel weights are nonnegative.
All inputs are finite; a program needn't handle non-finite values.
Results may differ from a plain program's by a relative error of at most 0.0015.
Values may be sent and summed in bfloat16 or wider, within the bound.
A program may use at most 128 MiB of HBM per device.

v0:
```python
import jax
import jax.numpy as jnp
from jax import lax
from jax.sharding import PartitionSpec as P

KSIDE = 9
COLS = 32


def with_halo(cells, sides, width):
    for axis, dim in sides:
        count = lax.axis_size(axis)
        ends = count - 1
        head = lax.slice_in_dim(cells, 0, width, axis=dim)
        tail = lax.slice_in_dim(cells, cells.shape[dim] - width, cells.shape[dim], axis=dim)
        cells = jnp.concatenate(
            [
                lax.ppermute(tail, axis, [(i, (i + 1) % count) for i in range(ends)]),
                cells,
                lax.ppermute(head, axis, [((i + 1) % count, i) for i in range(ends)]),
            ],
            axis=dim,
        )
    return cells


def stacked(flat, sign, axis, cols, cells):
    half = KSIDE // 2
    extended = jnp.pad(flat, ((0, 0), (half, half)))
    column = lax.iota(jnp.int32, cells) % cols
    pieces = []
    for shift_a in range(-half, half + 1):
        for shift_b in range(-half, half + 1):
            start = (half + sign * shift_a) * cols + half + sign * shift_b
            piece = extended[:, start : start + cells]
            moved = column + sign * shift_b
            keep = (moved >= 0) & (moved < cols)
            pieces.append(jnp.where(keep[None, :], piece, jnp.zeros_like(piece)))
    return jnp.stack(pieces, axis=axis)


def local(volume, kernel, measured):
    frames, local_depths, phases, cells = volume.shape
    cols = COLS
    half = KSIDE // 2
    offsets = kernel.shape[2]
    vol16 = volume.astype(jnp.bfloat16)
    rimmed = with_halo(vol16, (("tile", 3),), half * cols)
    partial_value = []
    for frame in range(frames):
        plane = 0
        flat = kernel[plane].reshape(phases, offsets * phases)
        spread = stacked(rimmed[frame, plane], 1, 0, cols, cells).reshape(offsets * phases, cells)
        total = jnp.dot(flat, spread, preferred_element_type=jnp.float32)
        partial_value.append(total)
    partial_value = jnp.stack(partial_value)
    projection = lax.psum(partial_value, "depth")
    ratio = (measured / projection).astype(jnp.bfloat16)
    ratio_rimmed = with_halo(ratio, (("tile", 2),), half * cols)
    spreads = [
        stacked(ratio_rimmed[frame], -1, 1, cols, cells).reshape(phases * offsets, cells)
        for frame in range(frames)
    ]
    plane = 0
    flat = kernel[plane].reshape(phases * offsets, phases)
    norm = jnp.sum(kernel[plane], axis=(0, 1), dtype=jnp.float32)
    backs = []
    for frame in range(frames):
        back = lax.dot_general(
            flat, spreads[frame], (((0,), (0,)), ((), ())), preferred_element_type=jnp.float32
        )
        backs.append(volume[frame, plane] * back / norm[:, None])
    planes = [jnp.stack(backs)]
    return jnp.stack(planes, axis=1)


def solution(mesh):
    in_specs = (P(None, "depth", None, "tile"), P("depth", None, None, None), P(None, None, "tile"))
    out_specs = P(None, "depth", None, "tile")
    return jax.shard_map(local, mesh=mesh, in_specs=in_specs, out_specs=out_specs, check_vma=False)
```

profile of v0, /device:TPU:1, one launch (start us, length us, event | category | flops | bytes accessed | tf_op | source)
XLA Modules:
  0.0 829.7 jit_solution(5707975148380617097)
XLA Ops:
  6.5 1.0 copy.22
  7.5 5.1 collective-permute-start.1
  12.6 3.0 collective-permute-start
  15.7 9.6 %copy.11 = bf16[1,225,81,225]{3,2,1,0:T(8,128)(2,1)} copy(bf16[1,225,81,225]{3,1,2,0:T(8,128)(2,1)} %param.4) | data formatting | bytes 16402500 | tf_op args[1]
  25.4 15.9 %reshape_squeeze.7 = bf16[225,18225]{1,0:T(8,128)(2,1)} reshape(bf16[1,225,81,225]{3,2,1,0:T(8,128)(2,1)} %copy.11) | data formatting | bytes 16402500 | tf_op jit(solution)/shard_map/reshape;squeeze | solution.py:52
  55.1 2.1 copy-done.1
  57.2 6.7 reshape.74
  114.9 6.8 reshape.75
  121.7 7.3 convolution_bitcast_fusion
  129.1 5.8 convolution_bitcast_fusion.1
  135.6 525.4 %all-reduce.6.cloned.1.call-done = f32[2,225,128]{2,1,0:T(8,128)} async-done(((f32[2,225,128]{2,1,0:T(8,128)}), f32[2,225,128]{2,1,0:T(8,128)}) %all-reduce.6.cloned.1.call-update) | async-done | bytes 230416 | tf_op jit(solution)/shard_map/psum | solution.py:57
  661.1 1.0 fusion.6
  662.1 31.6 %collective-permute-start.3 = (bf16[2,225,128]{2,1,0:T(8,128)(2,1)S(1)}, bf16[2,225,128]{2,1,0:T(8,128)(2,1)S(1)}, u32[]{:S(2)}, u32[]{:S(2)}) collective-permute-start(bf16[2,225,128]{2,1,0:T(8,128)(2,1)S(1)} %fusion.6), channel_id=1, source_target_pairs={{1,0},{2,1},{3,2},{5,4},{6,5},{7,6},{9,8},{10,9},{11,10},{13,12},{... | collective-permute-start | bytes 345608 | tf_op jit(solution)/shard_map/ppermute | solution.py:20
  693.6 4.2 collective-permute-start.2
  697.9 6.2 convert_reduce_fusion
  704.1 14.0 %reshape_squeeze.8 = bf16[18225,225]{1,0:T(8,128)(2,1)} reshape(bf16[1,225,81,225]{3,2,1,0:T(8,128)(2,1)} %copy.11) | data formatting | bytes 16402500 | tf_op jit(solution)/shard_map/reshape;squeeze | solution.py:65
  731.3 0.8 constant_dynamic-update-slice_fusion.162
  732.0 2.9 copy.13
  734.9 7.3 reshape.76
  793.1 5.3 copy.16
  798.4 7.4 reshape.77
  805.8 8.8 %fusion.3 = f32[1,225,128]{2,1,0:T(8,128)S(1)} fusion(bf16[18225,128]{1,0:T(8,128)(2,1)} %reshape.76, bf16[18225,225]{1,0:T(8,128)(2,1)} %reshape_squeeze.8, f32[2,1,225,128]{3,2,1,0:T(8,128)S(1)} %copy.9, f32[225]{0:T(256)S(1)} %convert_reduce_fusion), kind=kOutput, calls=%fused_computation.8 | convolution fusion | flops 1049817600 | bytes 13098150 | tf_op jit(solution)/shard_map/dot_general | solution.py:69
  814.6 7.3 fusion.5
  821.9 0.9 copy.17
  (339 shorter events, 129.0 us)
Async XLA Ops:
  6.5 654.5 %all-reduce.6.cloned.1.call-start = ((), (), s32[]{:S(2)}) async-start(), calls=%async_computation | async-start | bytes 475136 | tf_op jit(solution)/shard_map/psum | solution.py:57
  7.5 33.8 %collective-permute-start.1 = (bf16[2,1,225,128]{3,2,1,0:T(8,128)(2,1)S(1)}, bf16[2,1,225,128]{3,2,1,0:T(8,128)(2,1)S(1)}, u32[]{:S(2)}, u32[]{:S(2)}) collective-permute-start(bf16[2,1,225,128]{3,2,1,0:T(8,128)(2,1)S(1)} %copy.22), channel_id=1, source_target_pairs={{1,0},{2,1},{3,2},{5,4},{6,5},{7,6},{9,8},{10,9},{11,10},{13,12},{... | collective-permute-start | bytes 345608 | tf_op jit(solution)/shard_map/ppermute | solution.py:20
  12.6 28.6 %collective-permute-start = (bf16[2,1,225,128]{3,2,1,0:T(8,128)(2,1)S(1)}, bf16[2,1,225,128]{3,2,1,0:T(8,128)(2,1)S(1)}, u32[]{:S(2)}, u32[]{:S(2)}) collective-permute-start(bf16[2,1,225,128]{3,2,1,0:T(8,128)(2,1)S(1)} %copy.22), channel_id=1, source_target_pairs={{0,1},{1,2},{2,3},{4,5},{5,6},{6,7},{8,9},{9,10},{10,11},{12,13},{... | collective-permute-start | bytes 345608 | tf_op jit(solution)/shard_map/ppermute | solution.py:18
  55.1 2.1 copy-start.1
  114.9 14.2 %slice-start = ((s8[4667392]{0:T(1024)(128)(4,1)}), s8[473088]{0:T(1024)(128)(4,1)S(1)}, s32[]{:S(2)}) async-start(s8[4667392]{0:T(1024)(128)(4,1)} %bitcast.1350), calls=%async_computation.1 | async-start | bytes 946176
  121.7 7.3 slice-start.1
  129.1 532.0 %copy-start.3 = (f32[2,225,128]{2,0,1:T(2,128)S(1)}, f32[2,225,128]{2,0,1:T(2,128)}, u32[]{:S(2)}) copy-start(f32[2,225,128]{2,0,1:T(2,128)} %param.5) | copy-start | bytes 691204
  662.1 42.1 %copy-start.2 = (f32[2,1,225,128]{3,1,2,0:T(1,128)S(1)}, f32[2,1,225,128]{3,1,2,0:T(1,128)}, u32[]{:S(2)}) copy-start(f32[2,1,225,128]{3,1,2,0:T(1,128)} %param.3) | copy-start | bytes 691204
  662.1 56.1 %collective-permute-start.3 = (bf16[2,225,128]{2,1,0:T(8,128)(2,1)S(1)}, bf16[2,225,128]{2,1,0:T(8,128)(2,1)S(1)}, u32[]{:S(2)}, u32[]{:S(2)}) collective-permute-start(bf16[2,225,128]{2,1,0:T(8,128)(2,1)S(1)} %fusion.6), channel_id=1, source_target_pairs={{1,0},{2,1},{3,2},{5,4},{6,5},{7,6},{9,8},{10,9},{11,10},{13,12},{... | collective-permute-start | bytes 345608 | tf_op jit(solution)/shard_map/ppermute | solution.py:20
  693.6 24.5 %collective-permute-start.2 = (bf16[2,225,128]{2,1,0:T(8,128)(2,1)S(1)}, bf16[2,225,128]{2,1,0:T(8,128)(2,1)S(1)}, u32[]{:S(2)}, u32[]{:S(2)}) collective-permute-start(bf16[2,225,128]{2,1,0:T(8,128)(2,1)S(1)} %fusion.6), channel_id=1, source_target_pairs={{0,1},{1,2},{2,3},{4,5},{5,6},{6,7},{8,9},{9,10},{10,11},{12,13},{... | collective-permute-start | bytes 345608 | tf_op jit(solution)/shard_map/ppermute | solution.py:18
  805.8 8.8 %copy-start = (bf16[18225,128]{1,0:T(8,128)(2,1)S(1)}, bf16[18225,128]{1,0:T(8,128)(2,1)}, u32[]{:S(2)}) copy-start(bf16[18225,128]{1,0:T(8,128)(2,1)} %reshape.77) | copy-start | bytes 13996804
Sparse Core Ops, SparseCore 0:
  135.8 525.2 all-reduce.5
where the time goes:
time: 831 us; the launch traced here: 830 us
  waiting for transfers between devices  525 us (63%)
  other arithmetic  137 us (16%)
  local copies, waits for them, and re-layouts  80.1 us (10%)
  starting transfers between devices  43.9 us (5%)
  matrix products  29.3 us (4%)
  between operations  14.2 us (2%)
    psum x1, waiting for transfers between devices, local(): projection = lax.psum(partial_value, 'depth')  525 us
    unnamed x303, other arithmetic  126 us
    ppermute x2, starting transfers between devices, with_halo(): lax.ppermute(head, axis, [((i + 1) % count, i) for i in range(ends)])  36.7 us
  transfers between devices with their start and end apart: 5, of which 1 were waited for; matrix products, arithmetic and copies ran while one was open for 6% of the time, Pallas kernels for 0%

commit v1 on v0

--- a/solution.py
+++ b/solution.py
@@ -54,7 +54,7 @@
         total = jnp.dot(flat, spread, preferred_element_type=jnp.float32)
         partial_value.append(total)
     partial_value = jnp.stack(partial_value)
-    projection = lax.psum(partial_value, "depth")
+    projection = jnp.sum(lax.all_gather(partial_value, "depth"), axis=0)
     ratio = (measured / projection).astype(jnp.bfloat16)
     ratio_rimmed = with_halo(ratio, (("tile", 2),), half * cols)
     spreads = [

time: 831 us -> 617 us (0.74)
  waiting for transfers between devices: 525 us -> 285 us
  starting transfers between devices: 43.9 us -> 56 us
    psum x1 -> x0, waiting for transfers between devices: 525 us -> none  [local(): projection = lax.psum(partial_value, 'depth')]
    all_gather x0 -> x1, waiting for transfers between devices: none -> 285 us  [local(): projection = jnp.sum(lax.all_gather(partial_value, 'depth'), axis=0)]
    ppermute x2, starting transfers between devices: 36.7 us -> 50.1 us  [with_halo(): lax.ppermute(head, axis, [((i + 1) % count, i) for i in range(ends)])]
  transfers between devices with their start and end apart: 5 -> 5, of which waited for: 1 -> 1; matrix products, arithmetic and copies ran while one was open for 6% -> 8% of each run, Pallas kernels for 0% -> 0%
where the time goes in v1:
time: 617 us; the launch traced here: 607 us
  waiting for transfers between devices  285 us (46%)
  other arithmetic  142 us (23%)
  local copies, waits for them, and re-layouts  80.7 us (13%)
  starting transfers between devices  56 us (9%)
  matrix products  29.2 us (5%)
  between operations  14.4 us (2%)
    all_gather x1, waiting for transfers between devices, local(): projection = jnp.sum(lax.all_gather(partial_value, 'depth'), axis=0)  285 us
    unnamed x303, other arithmetic  126 us
    ppermute x2, starting transfers between devices, with_halo(): lax.ppermute(head, axis, [((i + 1) % count, i) for i in range(ends)])  50.1 us
    dot_general x2, matrix products, local(): lax.dot_general(flat, spreads[frame], (((0,), (0,)), ((), ())), preferred...  16.1 us
    another operation x1, local copies, waits for them, and re-layouts, local(): flat = kernel[plane].reshape(phases, offsets * phases)  15.9 us
    reshape x2, local copies, waits for them, and re-layouts, local(): stacked(ratio_rimmed[frame], -1, 1, cols, cells)  14.8 us
    another operation x1, local copies, waits for them, and re-layouts, local(): flat = kernel[plane].reshape(phases * offsets, phases)  14.2 us
    reshape x2, local copies, waits for them, and re-layouts, local(): stacked(rimmed[frame, plane], 1, 0, cols, cells)  13.8 us
  transfers between devices with their start and end apart: 5, of which 1 were waited for; matrix products, arithmetic and copies ran while one was open for 8% of the time, Pallas kernels for 0%

profile of v1, /device:TPU:1, one launch (start us, length us, event | category | flops | bytes accessed | tf_op | source)
XLA Modules:
  0.0 607.5 jit_solution(7642532097806532976)
XLA Ops:
  6.5 1.0 copy.31
  7.5 5.1 collective-permute-start.1
  12.6 3.0 collective-permute-start
  15.7 9.6 %copy.20 = bf16[1,225,81,225]{3,2,1,0:T(8,128)(2,1)} copy(bf16[1,225,81,225]{3,1,2,0:T(8,128)(2,1)} %param.4) | data formatting | bytes 16402500 | tf_op args[1]
  25.4 15.9 %reshape_squeeze.7 = bf16[225,18225]{1,0:T(8,128)(2,1)} reshape(bf16[1,225,81,225]{3,2,1,0:T(8,128)(2,1)} %copy.20) | data formatting | bytes 16402500 | tf_op jit(solution)/shard_map/reshape;squeeze | solution.py:52
  55.1 2.1 copy-done.1
  57.2 6.7 %reshape.74 = bf16[18225,128]{1,0:T(8,128)(2,1)} reshape(bf16[81,225,128]{2,1,0:T(8,128)(2,1)} %copy-done.1) | data formatting | bytes 9331200 | tf_op jit(solution)/shard_map/reshape | solution.py:53
  114.9 7.0 %reshape.75 = bf16[18225,128]{1,0:T(8,128)(2,1)} reshape(bf16[81,225,128]{2,1,0:T(8,128)(2,1)} %constant_dynamic-update-slice_fusion.81) | data formatting | bytes 9331200 | tf_op jit(solution)/shard_map/reshape | solution.py:53
  122.0 7.3 %convolution_bitcast_fusion = f32[1,225,128]{2,1,0:T(8,128)S(1)} fusion(bf16[18225,128]{1,0:T(8,128)(2,1)} %reshape.75, bf16[225,18225]{1,0:T(8,128)(2,1)} %reshape_squeeze.7), kind=kOutput, calls=%fused_computation.1 | convolution fusion | flops 1049760000 | bytes 12982050 | tf_op jit(solution)/shard_map/dot_general | solution.py:54
  129.3 5.8 convolution_bitcast_fusion.1
  135.9 285.1 %all-gather.3.cloned.1.call-done = f32[128,225,128]{2,1,0:T(8,128)} async-done(((f32[2,225,128]{2,1,0:T(8,128)}), f32[128,225,128]{2,1,0:T(8,128)}) %all-gather.3.cloned.1.call-update) | async-done | bytes 14745616 | tf_op jit(solution)/shard_map/all_gather | solution.py:57
  421.0 6.1 %reduce_sum.18 = f32[2,225,128]{2,1,0:T(8,128)S(1)} reduce(f32[64,2,225,128]{3,2,1,0:T(8,128)} %bitcast.1353, f32[]{:T(128)} %constant.48.clone.1), dimensions={0}, to_apply=%region_0.1 | reduce | flops 3628800 | bytes 14976004 | tf_op jit(solution)/shard_map/reduce_sum | solution.py:57
  427.2 44.9 %collective-permute-start.3 = (bf16[2,225,128]{2,1,0:T(8,128)(2,1)S(1)}, bf16[2,225,128]{2,1,0:T(8,128)(2,1)S(1)}, u32[]{:S(2)}, u32[]{:S(2)}) collective-permute-start(bf16[2,225,128]{2,1,0:T(8,128)(2,1)S(1)} %fusion.6), channel_id=1, source_target_pairs={{1,0},{2,1},{3,2},{5,4},{6,5},{7,6},{9,8},{10,9},{11,10},{13,12},{... | collective-permute-start | bytes 345608 | tf_op jit(solution)/shard_map/ppermute | solution.py:20
  472.1 2.9 collective-permute-start.2
  475.1 6.2 %convert_reduce_fusion = f32[225]{0:T(256)S(1)} fusion(bf16[1,225,81,225]{3,1,2,0:T(8,128)(2,1)} %param.4), kind=kLoop, calls=%fused_computation | loop fusion | flops 8201025 | bytes 8202150 | tf_op jit(solution)/shard_map/reduce_sum | solution.py:66
  481.3 14.2 %reshape_squeeze.8 = bf16[18225,225]{1,0:T(8,128)(2,1)} reshape(bf16[1,225,81,225]{3,2,1,0:T(8,128)(2,1)} %copy.20) | data formatting | bytes 16402500 | tf_op jit(solution)/shard_map/reshape;squeeze | solution.py:65
  508.7 0.8 constant_dynamic-update-slice_fusion.162
  509.4 2.9 copy.22
  512.3 7.3 %reshape.76 = bf16[18225,128]{1,0:T(8,128)(2,1)} reshape(bf16[225,81,128]{2,1,0:T(8,128)(2,1)} %copy.22) | data formatting | bytes 9331200 | tf_op jit(solution)/shard_map/reshape | solution.py:61
  570.5 5.3 copy.25
  575.8 7.5 %reshape.77 = bf16[18225,128]{1,0:T(8,128)(2,1)} reshape(bf16[225,81,128]{2,1,0:T(8,128)(2,1)} %copy.25) | data formatting | bytes 9331200 | tf_op jit(solution)/shard_map/reshape | solution.py:61
  583.3 8.8 %fusion.3 = f32[1,225,128]{2,1,0:T(8,128)S(1)} fusion(bf16[18225,128]{1,0:T(8,128)(2,1)} %reshape.76, bf16[18225,225]{1,0:T(8,128)(2,1)} %reshape_squeeze.8, f32[2,1,225,128]{3,2,1,0:T(8,128)S(1)} %copy.18, f32[225]{0:T(256)S(1)} %convert_reduce_fusion), kind=kOutput, calls=%fused_computation.8 | convolution fusion | flops 1049817600 | bytes 13098150 | tf_op jit(solution)/shard_map/dot_general | solution.py:69
  592.2 7.3 %fusion.5 = f32[1,225,128]{2,1,0:T(8,128)S(1)} fusion(bf16[18225,128]{1,0:T(8,128)(2,1)S(1)} %copy-done, bf16[18225,225]{1,0:T(8,128)(2,1)} %reshape_squeeze.8, f32[2,1,225,128]{3,2,1,0:T(8,128)S(1)} %copy.18, f32[225]{0:T(256)S(1)} %convert_reduce_fusion), kind=kOutput, calls=%fused_computation.10 | convolution fusion | flops 1049817600 | bytes 13098150 | tf_op jit(solution)/shard_map/dot_general | solution.py:69
  599.5 0.9 copy.26
  (340 shorter events, 129.1 us)
Async XLA Ops:
  6.5 414.5 %all-gather.3.cloned.1.call-start = ((), (), s32[]{:S(2)}) async-start(), calls=%async_computation | async-start | bytes 15441920 | tf_op jit(solution)/shard_map/all_gather | solution.py:57
  7.5 33.8 %collective-permute-start.1 = (bf16[2,1,225,128]{3,2,1,0:T(8,128)(2,1)S(1)}, bf16[2,1,225,128]{3,2,1,0:T(8,128)(2,1)S(1)}, u32[]{:S(2)}, u32[]{:S(2)}) collective-permute-start(bf16[2,1,225,128]{3,2,1,0:T(8,128)(2,1)S(1)} %copy.31), channel_id=1, source_target_pairs={{1,0},{2,1},{3,2},{5,4},{6,5},{7,6},{9,8},{10,9},{11,10},{13,12},{... | collective-permute-start | bytes 345608 | tf_op jit(solution)/shard_map/ppermute | solution.py:20
  12.6 28.6 %collective-permute-start = (bf16[2,1,225,128]{3,2,1,0:T(8,128)(2,1)S(1)}, bf16[2,1,225,128]{3,2,1,0:T(8,128)(2,1)S(1)}, u32[]{:S(2)}, u32[]{:S(2)}) collective-permute-start(bf16[2,1,225,128]{3,2,1,0:T(8,128)(2,1)S(1)} %copy.31), channel_id=1, source_target_pairs={{0,1},{1,2},{2,3},{4,5},{5,6},{6,7},{8,9},{9,10},{10,11},{12,13},{... | collective-permute-start | bytes 345608 | tf_op jit(solution)/shard_map/ppermute | solution.py:18
  55.1 2.1 copy-start.1
  114.9 14.4 %slice-start = ((s8[4667392]{0:T(1024)(128)(4,1)}), s8[473088]{0:T(1024)(128)(4,1)S(1)}, s32[]{:S(2)}) async-start(s8[4667392]{0:T(1024)(128)(4,1)} %bitcast.1351), calls=%async_computation.1 | async-start | bytes 946176
  121.9 7.4 %slice-start.1 = ((s8[4667392]{0:T(1024)(128)(4,1)}), s8[4194304]{0:T(1024)(128)(4,1)S(1)}, s32[]{:S(2)}) async-start(s8[4667392]{0:T(1024)(128)(4,1)} %bitcast.1351), calls=%async_computation.2 | async-start | bytes 8388608
  421.0 6.1 %copy-start.3 = (f32[2,225,128]{2,0,1:T(2,128)S(1)}, f32[2,225,128]{2,0,1:T(2,128)}, u32[]{:S(2)}) copy-start(f32[2,225,128]{2,0,1:T(2,128)} %param.5) | copy-start | bytes 691204
  427.1 54.2 %copy-start.2 = (f32[2,1,225,128]{3,1,2,0:T(1,128)S(1)}, f32[2,1,225,128]{3,1,2,0:T(1,128)}, u32[]{:S(2)}) copy-start(f32[2,1,225,128]{3,1,2,0:T(1,128)} %param.3) | copy-start | bytes 691204
  427.2 68.4 %collective-permute-start.3 = (bf16[2,225,128]{2,1,0:T(8,128)(2,1)S(1)}, bf16[2,225,128]{2,1,0:T(8,128)(2,1)S(1)}, u32[]{:S(2)}, u32[]{:S(2)}) collective-permute-start(bf16[2,225,128]{2,1,0:T(8,128)(2,1)S(1)} %fusion.6), channel_id=1, source_target_pairs={{1,0},{2,1},{3,2},{5,4},{6,5},{7,6},{9,8},{10,9},{11,10},{13,12},{... | collective-permute-start | bytes 345608 | tf_op jit(solution)/shard_map/ppermute | solution.py:20
  472.1 23.5 %collective-permute-start.2 = (bf16[2,225,128]{2,1,0:T(8,128)(2,1)S(1)}, bf16[2,225,128]{2,1,0:T(8,128)(2,1)S(1)}, u32[]{:S(2)}, u32[]{:S(2)}) collective-permute-start(bf16[2,225,128]{2,1,0:T(8,128)(2,1)S(1)} %fusion.6), channel_id=1, source_target_pairs={{0,1},{1,2},{2,3},{4,5},{5,6},{6,7},{8,9},{9,10},{10,11},{12,13},{... | collective-permute-start | bytes 345608 | tf_op jit(solution)/shard_map/ppermute | solution.py:18
  583.3 8.8 %copy-start = (bf16[18225,128]{1,0:T(8,128)(2,1)S(1)}, bf16[18225,128]{1,0:T(8,128)(2,1)}, u32[]{:S(2)}) copy-start(bf16[18225,128]{1,0:T(8,128)(2,1)} %reshape.77) | copy-start | bytes 13996804
Sparse Core Ops, SparseCore 0:
  136.0 284.9 all-gather.2
